TPU v7x, 128 devices: a whole 4x4x4 slice. The times are simulated.
128 devices in a mesh: row: 8 (over y, core), col: 16 (over x, z).
Axes of the slice: x: 4, y: 4, z: 4, core: 2. Of those that a mesh axis runs over, the one named last changes fastest.
Arguments:
- descriptors: bfloat16 [16384, 1024], P(('row', 'col'))
- gradients: bfloat16 [3, 4, 16384, 1024], P(None, None, ('row', 'col'))
- sparse_panel: bfloat16 [512, 1024], P('col')
- sparse_trail: bfloat16 [2048, 1024], P('col')
- atom_counts: int32 [128, 8], P(('row', 'col')), may hold values from 1 to 16, 64 in all within a row
- owner_rows: int32 [128, 8], P(('row', 'col')), may hold values from 0 to 7, each once within a row
- neighbor_ids: int32 [1024, 16, 4], P(('row', 'col')), may hold values from 0 to 65519
Outputs:
- panel_factor: float32 [512, 512], replicated
- cross_factor: float32 [2048, 512], P('col')
- trail_residual: float32 [2048, 65536], P('col', 'row')
Inputs may be any that keep to these rules, and one draw needn't show every extreme that they name: `atom_counts`: the structures of one device's line hold 64 atoms together, and every line has a structure of 16 atoms. `owner_rows`: every device gives exactly one structure to each row group.
All inputs are finite; a program needn't handle non-finite values.
Results may differ from a plain program's by a relative error of at most 0.0043.
Values may be sent and summed in bfloat16 or wider, within the bound.
No kernel may reach another device: no remote copies, remote signals or barrier semaphores. Data moves between devices by JAX's collectives and lax.ppermute only.
A program may use at most 128 MiB of HBM per device.

v0:
```python
import jax
import jax.numpy as jnp
from jax import lax
from jax.sharding import PartitionSpec as P

ridge_value = 0.1


def slot_rows(environments, desc_here, slope_here, count_here, neighbor_here, owner_here):
    struct_count = count_here.shape[0]
    atom_slots = neighbor_here.shape[1]
    neighbor_count = neighbor_here.shape[2]
    env_count = environments.shape[0]
    correlation = lax.dot_general(
        environments, desc_here, (((1,), (1,)), ((), ())), preferred_element_type=jnp.float32
    )
    slope_dots = lax.dot_general(
        environments, slope_here, (((1,), (1,)), ((), ())), preferred_element_type=jnp.float32
    )
    slope_dots = slope_dots.reshape(env_count, 3, neighbor_count, struct_count, atom_slots)
    slot_index = jnp.arange(atom_slots, dtype=jnp.int32)
    live_mask = (slot_index[None, :] < count_here[:, None]).astype(jnp.float32)
    squares = (correlation * correlation).reshape(env_count, struct_count, atom_slots)
    energy = jnp.sum(squares * live_mask[None], axis=2) / count_here.astype(jnp.float32)[None, :]
    partner = neighbor_here % count_here[:, None, None]
    struct_index = jnp.arange(struct_count, dtype=jnp.int32)
    flat_index = (struct_index[:, None, None] * atom_slots + partner).reshape(-1)
    picked = jnp.take(correlation, flat_index, axis=1).reshape(
        env_count, struct_count, atom_slots, neighbor_count
    )
    picked = jnp.transpose(picked, (0, 3, 1, 2))
    forces = -2.0 * jnp.sum(picked[:, None] * slope_dots, axis=2) * live_mask[None, None]
    forces = jnp.transpose(forces, (0, 2, 3, 1)).reshape(env_count, struct_count, 3 * atom_slots)
    padding = jnp.zeros((env_count, struct_count, atom_slots - 1), jnp.float32)
    slot_values = jnp.concatenate([energy[:, :, None], forces, padding], axis=2).astype(
        jnp.bfloat16
    )
    chosen = (owner_here[None, :] == struct_index[:, None]).astype(jnp.int32)
    owner_order = jnp.sum(struct_index[None, :] * chosen, axis=1)
    return jnp.take(slot_values, owner_order, axis=1)


def factor_panel(gram_sum, cross_sum, total_rows):
    gram_matrix = gram_sum / total_rows + ridge_value * jnp.eye(
        gram_sum.shape[0], dtype=jnp.float32
    )
    lower_factor = jnp.linalg.cholesky(gram_matrix)
    coupling = lax.linalg.triangular_solve(
        lower_factor, cross_sum / total_rows, left_side=True, lower=True
    )
    weights = lax.linalg.triangular_solve(
        lower_factor, coupling, left_side=True, lower=True, transpose_a=True
    )
    return (lower_factor.T, coupling, weights)


def split_weights(weights):
    weight_high = weights.astype(jnp.bfloat16)
    held_high = lax.optimization_barrier(weight_high)
    weight_low = (weights - held_high.astype(jnp.float32)).astype(jnp.bfloat16)
    return (weight_high, weight_low)


def reduce_products(gram_part, cross_part):
    return lax.psum((gram_part, cross_part), ("row", "col"))


def contract_rows(left_side, right_side):
    return lax.dot_general(
        left_side, right_side, (((1,), (1,)), ((), ())), preferred_element_type=jnp.float32
    )


def contract_cols(left_side, right_side):
    return lax.dot_general(
        left_side, right_side, (((0,), (0,)), ((), ())), preferred_element_type=jnp.float32
    )


def arrange_direct(block_rows, row_count, col_count):
    env_width = block_rows.shape[0] // col_count
    slot_count = block_rows.shape[2]
    shaped = block_rows.reshape(col_count, env_width, row_count, slot_count)
    return jnp.transpose(shaped, (2, 0, 1, 3)).reshape(row_count * col_count, env_width, slot_count)


def restore_direct(block_rows, row_count, col_count):
    env_width = block_rows.shape[1]
    slot_count = block_rows.shape[2]
    shaped = block_rows.reshape(row_count, col_count, env_width, slot_count)
    return jnp.transpose(shaped, (2, 1, 0, 3)).reshape(
        env_width, row_count * col_count * slot_count
    )


def per_device(
    descriptors, gradients, sparse_panel, sparse_trail, atom_counts, owner_rows, neighbor_ids
):
    row_count = lax.axis_size("row")
    col_count = lax.axis_size("col")
    col_index = lax.axis_index("col")
    count_here = atom_counts[0]
    owner_here = owner_rows[0]
    slope_here = gradients.reshape(-1, gradients.shape[3])
    panel_width = sparse_panel.shape[0]
    trail_width = sparse_trail.shape[0]
    panel_total = panel_width * col_count
    trail_total = trail_width * col_count
    slot_count = 4 * neighbor_ids.shape[1]
    total_rows = row_count * row_count * col_count * slot_count
    own_envs = jnp.concatenate([sparse_panel, sparse_trail], axis=0)
    kernel_rows = slot_rows(
        lax.all_gather(own_envs, "col", axis=0, tiled=True),
        descriptors,
        slope_here,
        count_here,
        neighbor_ids,
        owner_here,
    )
    blocks = kernel_rows.reshape(col_count, panel_width + trail_width, row_count, slot_count)
    panel_rows = blocks[:, :panel_width].reshape(panel_total, row_count, slot_count)
    trail_rows = blocks[:, panel_width:].reshape(trail_total, row_count, slot_count)
    received = (
        lax.all_to_all(
            arrange_direct(panel_rows, row_count, col_count),
            ("row", "col"),
            split_axis=0,
            concat_axis=0,
            tiled=True,
        ),
        lax.all_to_all(
            arrange_direct(trail_rows, row_count, col_count),
            ("row", "col"),
            split_axis=0,
            concat_axis=0,
            tiled=True,
        ),
    )
    panel_own = restore_direct(received[0], row_count, col_count)
    trail_own = restore_direct(received[1], row_count, col_count)
    segment = lax.all_gather(panel_own, "col", axis=0, tiled=True)
    columns = jnp.concatenate(
        [contract_rows(segment, panel_own), contract_rows(segment, trail_own)], axis=1
    )
    gram_part = lax.dynamic_update_slice(
        jnp.zeros((panel_total, panel_total), jnp.float32),
        columns[:, :panel_width],
        (0, col_index * panel_width),
    )
    cross_part = lax.dynamic_update_slice(
        jnp.zeros((panel_total, trail_total), jnp.float32),
        columns[:, panel_width:],
        (0, col_index * trail_width),
    )
    gram_sum, cross_sum = reduce_products(gram_part, cross_part)
    panel_factor, coupling, weights = factor_panel(gram_sum, cross_sum, total_rows)
    coupling_own = lax.dynamic_slice_in_dim(coupling, col_index * trail_width, trail_width, 1)
    weights_own = lax.dynamic_slice_in_dim(weights, col_index * trail_width, trail_width, 1)
    weight_high, weight_low = split_weights(weights_own)
    segment = lax.all_gather(panel_own, "col", axis=0, tiled=True)
    trail_residual = (
        trail_own.astype(jnp.float32)
        - contract_cols(weight_high, segment)
        - contract_cols(weight_low, segment)
    )
    cross_factor = coupling_own.T
    return (panel_factor, cross_factor, trail_residual)


def solution(mesh):
    return jax.shard_map(
        per_device,
        mesh=mesh,
        in_specs=(
            P(("row", "col"), None),
            P(None, None, ("row", "col"), None),
            P("col", None),
            P("col", None),
            P(("row", "col"), None),
            P(("row", "col"), None),
            P(("row", "col"), None, None),
        ),
        out_specs=(P(), P("col", None), P("col", "row")),
        check_vma=False,
    )
```

profile of v0, /device:TPU:1, one launch (start us, length us, event | category | flops | bytes accessed | tf_op | source)
XLA Modules:
  0.0 593.3 jit_solution(4389010923176962485)
XLA Ops:
  7.2 1.8 pad_maximum_fusion
  14.9 55.6 %all-gather.3.cloned.1.call-done = bf16[2560,1024]{1,0:T(8,128)(2,1)} async-done(((bf16[160,1024]{1,0:T(8,128)(2,1)}), bf16[2560,1024]{1,0:T(8,128)(2,1)}) %all-gather.3.cloned.1.call-update) | async-done | bytes 5242896 | tf_op jit(solution)/shard_map/all_gather | solution.py:113
  70.5 5.5 multiply_reduce_fusion.1
  75.9 7.7 %gather_fusion = f32[512,2560]{1,0:T(8,128)} fusion(f32[2560,128]{0,1:T(8,128)} %get-tuple-element.64, s32[1024]{0:T(1024)S(1)} %pad_clamp_fusion.1), kind=kCustom, calls=%fused_computation | custom fusion | bytes 10487808 | tf_op jit(solution)/shard_map/jit(_take)/gather | solution.py:28
  83.6 7.1 %gather.17 = f32[2560,8,16,4]{0,3,2,1:T(4,128)} reshape(f32[2560,512]{0,1:T(8,128)} %bitcast.121) | data formatting | bytes 10485760 | tf_op jit(solution)/shard_map/jit(_take)/gather | solution.py:28
  90.7 4.6 fusion.1
  95.4 12.1 %multiply_reduce_fusion = f32[2560,3,8,16]{0,3,2,1:T(8,128)S(1)} fusion(f32[2560,4,8,16]{0,3,2,1:T(8,128)S(1)} %fusion.1, bf16[3,4,8,16,1024]{4,3,2,1,0:T(8,128)(2,1)S(1)} %bitcast.117, bf16[2560,1024]{1,0:T(8,128)(2,1)} %all-gather.3.cloned.1.call-done), kind=kOutput, calls=%fused_computation.4 | convolution fusion | flops 8059944960 | bytes 17563648 | tf_op jit(solution)/shard_map/dot_general | solution.py:17
  110.6 2.2 gather_fusion.1
  112.8 8.5 %gather.19 = bf16[16,160,8,64]{1,0,3,2:T(8,128)(2,1)} reshape(bf16[2560,8,64]{0,2,1:T(8,128)(2,1)} %bitcast.120) | data formatting | bytes 5242880 | tf_op jit(solution)/shard_map/jit(_take)/gather | solution.py:40
  121.2 3.6 copy_select_fusion.1
  124.9 2.0 copy-done.5
  128.9 21.1 %all_to_all.10 = bf16[128,2,1024]{2,1,0:T(2,128)(2,1)S(1)} all-to-all(bf16[128,2,1024]{2,1,0:T(2,128)(2,1)S(1)} %reshape.290), channel_id=1, replica_groups=mesh['row'=8,'col'=16] {'row','col'}, dimensions={0} | all-to-all | bytes 1048576 | tf_op jit(solution)/shard_map/all_to_all | solution.py:124
  151.3 1.6 reshape.250
  152.9 4.3 slice.149
  157.3 4.8 all-to-all-start.1
  162.2 36.1 %all-to-all-done.1 = bf16[128,128,64]{1,2,0:T(8,128)(2,1)S(1)} async-done(((bf16[128,128,64]{1,2,0:T(8,128)(2,1)}), bf16[128,128,64]{1,2,0:T(8,128)(2,1)S(1)}, u32[]{:S(2)}, u32[]{:S(2)}) %all-to-all-start.1) | async-done | bytes 2097184 | tf_op jit(solution)/shard_map/all_to_all | solution.py:131
  198.3 1.6 copy.80
  199.9 40.1 %all-gather.5.cloned.1.call-done = bf16[512,8192]{1,0:T(8,128)(2,1)} async-done(((bf16[32,8192]{1,0:T(8,128)(2,1)}), bf16[512,8192]{1,0:T(8,128)(2,1)}) %all-gather.5.cloned.1.call-update) | async-done | bytes 8388624 | tf_op jit(solution)/shard_map/all_gather | solution.py:141
  240.1 6.1 %convolution_dynamic-update-slice_fusion.3 = f32[512,512]{0,1:T(8,128)S(1)} fusion(f32[512,512]{0,1:T(8,128)S(1)} %broadcast_in_dim.40, s32[]{:T(128)S(6)} %select_n.80, bf16[512,8192]{1,0:T(8,128)(2,1)} %all-gather.5.cloned.1.call-done, bf16[32,8192]{1,0:T(8,128)(2,1)S(1)} %copy-done.8), kind=kOutput, calls=%fused_computation.54 | convolution fusion | flops 268435456 | bytes 8978436 | tf_op jit(solution)/shard_map/dot_general | solution.py:69
  247.2 2.5 broadcast_in_dim.46
  249.8 3.1 convolution_dynamic-update-slice_fusion
  252.9 3.4 copy.81
  256.2 152.8 %all-reduce.4.cloned.1.call-done = (f32[512,512]{0,1:T(8,128)}, f32[512,2048]{1,0:T(8,128)}) async-done(((f32[512,512]{0,1:T(8,128)}, f32[512,2048]{1,0:T(8,128)}), (f32[512,512]{0,1:T(8,128)}, f32[512,2048]{1,0:T(8,128)})) %all-reduce.4.cloned.1.call-update) | async-done | bytes 5242896 | tf_op jit(solution)/shard_map/psum | solution.py:65
  409.0 1.4 select_add_fusion
  411.1 11.7 %cholesky.103 = f32[128,128]{1,0:T(8,128)S(1)} custom-call(f32[128,128]{1,0:T(8,128)S(1)} %cholesky.263), custom_call_target="Cholesky" | custom-call | tf_op jit(solution)/shard_map/jit(cholesky)/cholesky | solution.py:47
  423.0 9.8 %custom-call.32 = f32[1,128,128]{1,2,0:T(8,128)S(1)} custom-call(f32[1,128,128]{2,1,0:T(8,128)S(1)} %get-tuple-element.62), custom_call_target="InvertDiagBlocksLowerTriangular" | custom-call | tf_op jit(solution)/shard_map/jit(cholesky)/cholesky | solution.py:47
  433.6 11.7 %cholesky.215 = f32[128,128]{1,0:T(8,128)S(1)} custom-call(f32[128,128]{1,0:T(8,128)S(1)} %cholesky.267), custom_call_target="Cholesky" | custom-call | tf_op jit(solution)/shard_map/jit(cholesky)/cholesky | solution.py:47
  445.6 10.0 %custom-call.33 = f32[1,128,128]{1,2,0:T(8,128)S(1)} custom-call(f32[1,128,128]{2,1,0:T(8,128)S(1)} %get-tuple-element.60), custom_call_target="InvertDiagBlocksLowerTriangular" | custom-call | tf_op jit(solution)/shard_map/jit(cholesky)/cholesky | solution.py:47
  456.5 11.7 %cholesky.236 = f32[128,128]{1,0:T(8,128)S(1)} custom-call(f32[128,128]{1,0:T(8,128)S(1)} %cholesky.272), custom_call_target="Cholesky" | custom-call | tf_op jit(solution)/shard_map/jit(cholesky)/cholesky | solution.py:47
  468.4 9.8 %custom-call.34 = f32[1,128,128]{1,2,0:T(8,128)S(1)} custom-call(f32[1,128,128]{2,1,0:T(8,128)S(1)} %get-tuple-element.58), custom_call_target="InvertDiagBlocksLowerTriangular" | custom-call | tf_op jit(solution)/shard_map/jit(cholesky)/cholesky | solution.py:47
  479.0 11.9 %cholesky.253 = f32[128,128]{1,0:T(8,128)S(1)} custom-call(f32[128,128]{1,0:T(8,128)S(1)} %convolution_subtract_fusion.8), custom_call_target="Cholesky" | custom-call | tf_op jit(solution)/shard_map/jit(cholesky)/cholesky | solution.py:47
  493.7 4.8 broadcast_multiply_fusion
  502.3 11.1 %while.1 = (s32[]{:T(128)}, f32[512,512]{0,1:T(8,128)S(1)}, s32[4,2]{0,1:T(2,128)S(1)}, f32[4,128,128]{2,1,0:T(8,128)}, s32[]{:T(128)}) while((s32[]{:T(128)}, f32[512,512]{0,1:T(8,128)S(1)}, s32[4,2]{0,1:T(2,128)S(1)}, f32[4,128,128]{2,1,0:T(8,128)}, s32[]{:T(128)}) %tuple.40), condition=%wide.while_cond, body=%wide.while_body.sunk | while | flops 2 | bytes 393329 | solution.py:48
  503.0 1.4 dynamic-slice.7
  505.8 1.4 dynamic-slice.7
  508.6 1.4 dynamic-slice.7
  511.4 1.4 dynamic-slice.7
  513.5 40.2 %custom-call.35 = f32[4,128,128]{1,2,0:T(8,128)S(1)} custom-call(f32[4,128,128]{2,1,0:T(8,128)} %get-tuple-element.10), custom_call_target="InvertDiagBlocksLowerTriangular" | custom-call | tf_op jit(solution)/shard_map/triangular_solve | solution.py:48
  553.7 2.4 fusion.27
  556.1 2.3 convolution_subtract_fusion.5
  559.5 1.3 convolution_subtract_fusion.3
  561.8 3.2 fusion.17
  567.8 1.8 copy.82
  569.6 2.3 convolution_subtract_fusion.4
  572.9 2.6 convolution_subtract_fusion.2
  576.5 3.1 fusion.14
  581.2 1.4 convolution_subtract_fusion.1
  582.7 3.6 convolution_subtract_fusion
  (119 shorter events, 35.0 us)
Async XLA Ops:
  7.2 88.2 %copy-start = (bf16[3,4,128,1024]{3,2,1,0:T(8,128)(2,1)S(1)}, bf16[3,4,128,1024]{3,2,1,0:T(8,128)(2,1)}, u32[]{:S(2)}) copy-start(bf16[3,4,128,1024]{3,2,1,0:T(8,128)(2,1)} %param.8) | copy-start | bytes 9437188
  7.2 63.3 %all-gather.3.cloned.1.call-start = ((), (), s32[]{:S(2)}) async-start(), calls=%async_computation.2 | async-start | bytes 5570560 | tf_op jit(solution)/shard_map/all_gather | solution.py:113
  9.1 230.9 %all-gather.5.cloned.1.call-start = ((), (), s32[]{:S(2)}) async-start(), calls=%async_computation.3 | async-start | bytes 8912896 | tf_op jit(solution)/shard_map/all_gather | solution.py:141
  124.9 2.0 copy-start.5
  157.3 82.8 %copy-start.8 = (bf16[32,8192]{1,0:T(8,128)(2,1)S(1)}, bf16[32,8192]{1,0:T(8,128)(2,1)}, u32[]{:S(2)}) copy-start(bf16[32,8192]{1,0:T(8,128)(2,1)} %reshape.250) | copy-start | bytes 1572868
  157.3 41.0 %all-to-all-start.1 = ((bf16[128,128,64]{1,2,0:T(8,128)(2,1)}), bf16[128,128,64]{1,2,0:T(8,128)(2,1)S(1)}, u32[]{:S(2)}, u32[]{:S(2)}) async-start(bf16[128,128,64]{1,2,0:T(8,128)(2,1)} %bitcast.123), calls=%async_computation.1 | async-start | bytes 4194304 | tf_op jit(solution)/shard_map/all_to_all | solution.py:131
  162.1 246.9 %all-reduce.4.cloned.1.call-start = ((), (), s32[]{:S(2)}) async-start(), calls=%async_computation.4 | async-start | bytes 10485760 | tf_op jit(solution)/shard_map/psum | solution.py:65
  240.1 9.7 %copy-start.2 = (bf16[512,8192]{1,0:T(8,128)(2,1)S(1)}, bf16[512,8192]{1,0:T(8,128)(2,1)}, u32[]{:S(2)}) copy-start(bf16[512,8192]{1,0:T(8,128)(2,1)} %all-gather.5.cloned.1.call-done) | copy-start | bytes 25165828
  246.2 1.0 copy-start.11
  247.2 2.5 copy-start.7
  409.0 1.8 copy-start.10
  513.5 45.9 %copy-start.9 = (f32[512,512]{0,1:T(8,128)}, f32[512,512]{0,1:T(8,128)S(1)}, u32[]{:S(2)}) copy-start(f32[512,512]{0,1:T(8,128)S(1)} %get-tuple-element.126) | copy-start | bytes 3145732
  553.7 5.8 copy-start.4
  561.8 4.3 copy-start.3
  572.9 7.8 %slice-start = ((s8[8388608]{0:T(1024)(128)(4,1)}), s8[4194304]{0:T(1024)(128)(4,1)S(1)}, s32[]{:S(2)}) async-start(s8[8388608]{0:T(1024)(128)(4,1)} %bitcast.118), calls=%async_computation.5 | async-start | bytes 8388608
  576.5 4.2 slice-start.1
  579.6 1.6 copy-start.6
  582.7 3.6 copy-start.1
Sparse Core Ops, SparseCore 0:
  10.8 59.6 all-gather.2
  153.0 86.8 all-gather.4
  253.0 156.0 all-reduce.3
where the time goes:
time: 604 us; the launch traced here: 593 us
  waiting for transfers between devices  285 us (47%)
  other arithmetic  145 us (24%)
  local copies, waits for them, and re-layouts  61.7 us (10%)
  matrix products  58.4 us (10%)
  blocking collectives  21.1 us (3%)
  between operations  17.4 us (3%)
    psum x1, waiting for transfers between devices, reduce_products(): return lax.psum((gram_part, cross_part), ('row', 'col'))  153 us
    another operation x15, other arithmetic, factor_panel(): lower_factor = jnp.linalg.cholesky(gram_matrix)  79.5 us
    all_gather x1, waiting for transfers between devices, per_device(): lax.all_gather(own_envs, 'col', axis=0, tiled=True)  55.6 us
    another operation x3, other arithmetic, factor_panel(): lax.linalg.triangular_solve(lower_factor, cross_sum / total_rows, left_si...  41.4 us
    all_gather x1, waiting for transfers between devices, per_device(): segment = lax.all_gather(panel_own, 'col', axis=0, tiled=True)  40.1 us
    all_to_all x1, waiting for transfers between devices, per_device(): lax.all_to_all(arrange_direct(trail_rows, row_count, col_count), ('row',...  36.1 us
    all_to_all x1, blocking collectives, per_device(): lax.all_to_all(arrange_direct(panel_rows, row_count, col_count), ('row',...  21.1 us
    gather x2, local copies, waits for them, and re-layouts, slot_rows(): jnp.take(correlation, flat_index, axis=1)  14.8 us
  transfers between devices with their start and end apart: 4, of which 4 were waited for; matrix products, arithmetic and copies ran while one was open for 3% of the time, Pallas kernels for 0%

commit v1 on v0

--- a/solution.py
+++ b/solution.py
@@ -138,7 +138,22 @@
     )
     panel_own = restore_direct(received[0], row_count, col_count)
     trail_own = restore_direct(received[1], row_count, col_count)
-    segment = lax.all_gather(panel_own, "col", axis=0, tiled=True)
+    ways, here, step = (lax.axis_size("col"), lax.axis_index("col"), panel_own.shape[0])
+    shape = [n * ways if d == 0 else n for d, n in enumerate(panel_own.shape)]
+    segment = lax.dynamic_update_slice_in_dim(
+        jnp.zeros(shape, panel_own.dtype), panel_own, here * step, axis=0
+    )
+    going_up = going_down = panel_own
+    for far in range(1, ways // 2 + 1):
+        going_up = lax.ppermute(going_up, "col", [(d, (d + 1) % ways) for d in range(ways)])
+        segment = lax.dynamic_update_slice_in_dim(
+            segment, going_up, (here - far) % ways * step, axis=0
+        )
+        if 2 * far < ways:
+            going_down = lax.ppermute(going_down, "col", [(d, (d - 1) % ways) for d in range(ways)])
+            segment = lax.dynamic_update_slice_in_dim(
+                segment, going_down, (here + far) % ways * step, axis=0
+            )
     columns = jnp.concatenate(
         [contract_rows(segment, panel_own), contract_rows(segment, trail_own)], axis=1
     )

time: 604 us -> 658 us (1.089)
  starting transfers between devices: 4.96 us -> 47.3 us
  local copies, waits for them, and re-layouts: 61.7 us -> 87.9 us
  blocking collectives: 21.1 us -> 0 us
    ppermute x0 -> x15, waiting for transfers between devices: none -> 70.7 us  [the longest x8 70.6 us: per_device(): lax.ppermute(going_up, 'col', [(d, (d + 1) % ways) for d in range(ways)])]
    all_gather x1, waiting for transfers between devices: 40.1 us -> 0.01 us  [per_device(): segment = lax.all_gather(panel_own, 'col', axis=0, tiled=True)]
    all_to_all x1, waiting for transfers between devices: 36.1 us -> 0.01 us  [per_device(): lax.all_to_all(arrange_direct(trail_rows, row_count, col_count), ('row',...]
    ppermute x0 -> x15, starting transfers between devices: none -> 34.6 us  [the longest x7 32.7 us: per_device(): lax.ppermute(going_down, 'col', [(d, (d - 1) % ways) for d in range(ways)])]
    all_to_all x1 -> x0, blocking collectives: 21.1 us -> none  [per_device(): lax.all_to_all(arrange_direct(panel_rows, row_count, col_count), ('row',...]
    dynamic_update_slice x0 -> x16, local copies, waits for them, and re-layouts: none -> 16.5 us  [the longest x8 8.81 us: per_device(): lax.dynamic_update_slice_in_dim(segment, going_up, (here - far) % ways *...]
    all_to_all x0 -> x1, waiting for transfers between devices: none -> 8.77 us  [per_device(): lax.all_to_all(arrange_direct(panel_rows, row_count, col_count), ('row',...]
    all_to_all x0 -> x1, starting transfers between devices: none -> 7.87 us  [per_device(): lax.all_to_all(arrange_direct(panel_rows, row_count, col_count), ('row',...]
  transfers between devices with their start and end apart: 4 -> 20, of which waited for: 4 -> 11; matrix products, arithmetic and copies ran while one was open for 3% -> 31% of each run, Pallas kernels for 0% -> 0%
where the time goes in v1:
time: 658 us; the launch traced here: 647 us
  waiting for transfers between devices  291 us (44%)
  other arithmetic  142 us (22%)
  local copies, waits for them, and re-layouts  87.9 us (13%)
  matrix products  61.4 us (9%)
  starting transfers between devices  47.3 us (7%)
  between operations  17.7 us (3%)
    psum x1, waiting for transfers between devices, reduce_products(): return lax.psum((gram_part, cross_part), ('row', 'col'))  155 us
    another operation x15, other arithmetic, factor_panel(): lower_factor = jnp.linalg.cholesky(gram_matrix)  79.3 us
    ppermute x8, waiting for transfers between devices, per_device(): lax.ppermute(going_up, 'col', [(d, (d + 1) % ways) for d in range(ways)])  70.6 us
    all_gather x1, waiting for transfers between devices, per_device(): lax.all_gather(own_envs, 'col', axis=0, tiled=True)  55.7 us
    another operation x3, other arithmetic, factor_panel(): lax.linalg.triangular_solve(lower_factor, cross_sum / total_rows, left_si...  41.4 us
    ppermute x7, starting transfers between devices, per_device(): lax.ppermute(going_down, 'col', [(d, (d - 1) % ways) for d in range(ways)])  32.7 us
    gather x2, local copies, waits for them, and re-layouts, slot_rows(): jnp.take(correlation, flat_index, axis=1)  14.8 us
  transfers between devices with their start and end apart: 20, of which 11 were waited for; matrix products, arithmetic and copies ran while one was open for 31% of the time, Pallas kernels for 0%

profile of v1, /device:TPU:1, one launch (start us, length us, event | category | flops | bytes accessed | tf_op | source)
XLA Modules:
  0.0 646.9 jit_solution(4234838282801540895)
XLA Ops:
  14.8 55.7 %all-gather.3.cloned.1.call-done = bf16[2560,1024]{1,0:T(8,128)(2,1)} async-done(((bf16[160,1024]{1,0:T(8,128)(2,1)}), bf16[2560,1024]{1,0:T(8,128)(2,1)}) %all-gather.3.cloned.1.call-update) | async-done | bytes 5242896 | tf_op jit(solution)/shard_map/all_gather | solution.py:113
  70.5 5.5 multiply_reduce_fusion.1
  75.9 7.7 %gather_fusion = f32[512,2560]{1,0:T(8,128)} fusion(f32[2560,128]{0,1:T(8,128)} %get-tuple-element.71, s32[1024]{0:T(1024)S(1)} %pad_clamp_fusion.1), kind=kCustom, calls=%fused_computation | custom fusion | bytes 10487808 | tf_op jit(solution)/shard_map/jit(_take)/gather | solution.py:28
  83.6 7.1 %gather.17 = f32[2560,8,16,4]{0,3,2,1:T(4,128)} reshape(f32[2560,512]{0,1:T(8,128)} %bitcast.118) | data formatting | bytes 10485760 | tf_op jit(solution)/shard_map/jit(_take)/gather | solution.py:28
  90.7 4.6 fusion.1
  95.4 12.1 %multiply_reduce_fusion = f32[2560,3,8,16]{0,3,2,1:T(8,128)S(1)} fusion(f32[2560,4,8,16]{0,3,2,1:T(8,128)S(1)} %fusion.1, bf16[3,4,8,16,1024]{4,3,2,1,0:T(8,128)(2,1)S(1)} %bitcast.116, bf16[2560,1024]{1,0:T(8,128)(2,1)} %all-gather.3.cloned.1.call-done), kind=kOutput, calls=%fused_computation.4 | convolution fusion | flops 8059944960 | bytes 17563648 | tf_op jit(solution)/shard_map/dot_general | solution.py:17
  112.8 8.5 %gather.19 = bf16[16,160,8,64]{1,0,3,2:T(8,128)(2,1)} reshape(bf16[2560,8,64]{0,2,1:T(8,128)(2,1)} %bitcast.117) | data formatting | bytes 5242880 | tf_op jit(solution)/shard_map/jit(_take)/gather | solution.py:40
  121.2 3.6 copy_select_fusion.1
  129.7 7.9 %all-to-all-start = ((bf16[128,2,1024]{2,1,0:T(2,128)(2,1)}), bf16[128,2,1024]{2,1,0:T(2,128)(2,1)S(1)}, u32[]{:S(2)}, u32[]{:S(2)}) async-start(bf16[128,2,1024]{2,1,0:T(2,128)(2,1)} %reshape.290), calls=%async_computation | async-start | bytes 1048576 | tf_op jit(solution)/shard_map/all_to_all | solution.py:124
  137.9 4.4 slice.149
  142.2 8.8 %all-to-all-done = bf16[128,2,1024]{2,1,0:T(2,128)(2,1)S(1)} async-done(((bf16[128,2,1024]{2,1,0:T(2,128)(2,1)}), bf16[128,2,1024]{2,1,0:T(2,128)(2,1)S(1)}, u32[]{:S(2)}, u32[]{:S(2)}) %all-to-all-start) | async-done | bytes 524320 | tf_op jit(solution)/shard_map/all_to_all | solution.py:124
  151.0 4.7 all-to-all-start.1
  157.3 2.9 copy.89
  164.0 4.0 collective-permute-start.1
  168.0 4.2 broadcast_in_dim.44
  173.1 23.2 %collective-permute-done = bf16[32,8192]{1,0:T(8,128)(2,1)S(1)} collective-permute-done((bf16[32,8192]{1,0:T(8,128)(2,1)S(1)}, bf16[32,8192]{1,0:T(8,128)(2,1)S(1)}, u32[]{:S(2)}, u32[]{:S(2)}) %collective-permute-start) | collective-permute-done | bytes 524320 | tf_op jit(solution)/shard_map/ppermute | solution.py:148
  196.3 4.8 collective-permute-start.3
  202.8 9.6 %collective-permute-done.2 = bf16[32,8192]{1,0:T(8,128)(2,1)} collective-permute-done((bf16[32,8192]{1,0:T(8,128)(2,1)S(1)}, bf16[32,8192]{1,0:T(8,128)(2,1)}, u32[]{:S(2)}, u32[]{:S(2)}) %collective-permute-start.2) | collective-permute-done | bytes 524320 | tf_op jit(solution)/shard_map/ppermute | solution.py:148
  212.4 4.8 collective-permute-start.5
  223.1 4.7 collective-permute-done.4
  228.0 4.8 collective-permute-start.7
  236.5 5.8 collective-permute-done.6
  242.4 4.8 collective-permute-start.9
  248.8 6.8 %collective-permute-done.8 = bf16[32,8192]{1,0:T(8,128)(2,1)S(1)} collective-permute-done((bf16[32,8192]{1,0:T(8,128)(2,1)S(1)}, bf16[32,8192]{1,0:T(8,128)(2,1)S(1)}, u32[]{:S(2)}, u32[]{:S(2)}) %collective-permute-start.8) | collective-permute-done | bytes 524320 | tf_op jit(solution)/shard_map/ppermute | solution.py:148
  255.6 4.8 collective-permute-start.11
  262.1 5.9 collective-permute-done.10
  267.9 4.8 collective-permute-start.13
  274.4 4.9 collective-permute-done.12
  280.9 9.8 %collective-permute-done.14 = bf16[32,8192]{1,0:T(8,128)(2,1)S(1)} collective-permute-done((bf16[32,8192]{1,0:T(8,128)(2,1)S(1)}, bf16[32,8192]{1,0:T(8,128)(2,1)S(1)}, u32[]{:S(2)}, u32[]{:S(2)}) %collective-permute-start.14) | collective-permute-done | bytes 524320 | tf_op jit(solution)/shard_map/ppermute | solution.py:148
  291.7 6.0 convolution_dynamic-update-slice_fusion.3
  298.6 2.5 broadcast_in_dim.50
  301.2 6.4 convolution_dynamic-update-slice_fusion
  308.4 3.3 copy.100
  311.7 154.9 %all-reduce.4.cloned.1.call-done = (f32[512,512]{0,1:T(8,128)}, f32[512,2048]{1,0:T(8,128)}) async-done(((f32[512,512]{0,1:T(8,128)}, f32[512,2048]{1,0:T(8,128)}), (f32[512,512]{0,1:T(8,128)}, f32[512,2048]{1,0:T(8,128)})) %all-reduce.4.cloned.1.call-update) | async-done | bytes 5242896 | tf_op jit(solution)/shard_map/psum | solution.py:65
  468.6 11.7 %cholesky.103 = f32[128,128]{1,0:T(8,128)S(1)} custom-call(f32[128,128]{1,0:T(8,128)S(1)} %cholesky.263), custom_call_target="Cholesky" | custom-call | tf_op jit(solution)/shard_map/jit(cholesky)/cholesky | solution.py:47
  480.5 9.8 %custom-call.32 = f32[1,128,128]{1,2,0:T(8,128)S(1)} custom-call(f32[1,128,128]{2,1,0:T(8,128)S(1)} %get-tuple-element.69), custom_call_target="InvertDiagBlocksLowerTriangular" | custom-call | tf_op jit(solution)/shard_map/jit(cholesky)/cholesky | solution.py:47
  491.1 11.7 %cholesky.215 = f32[128,128]{1,0:T(8,128)S(1)} custom-call(f32[128,128]{1,0:T(8,128)S(1)} %cholesky.267), custom_call_target="Cholesky" | custom-call | tf_op jit(solution)/shard_map/jit(cholesky)/cholesky | solution.py:47
  503.1 10.0 %custom-call.33 = f32[1,128,128]{1,2,0:T(8,128)S(1)} custom-call(f32[1,128,128]{2,1,0:T(8,128)S(1)} %get-tuple-element.67), custom_call_target="InvertDiagBlocksLowerTriangular" | custom-call | tf_op jit(solution)/shard_map/jit(cholesky)/cholesky | solution.py:47
  514.0 11.7 %cholesky.236 = f32[128,128]{1,0:T(8,128)S(1)} custom-call(f32[128,128]{1,0:T(8,128)S(1)} %cholesky.272), custom_call_target="Cholesky" | custom-call | tf_op jit(solution)/shard_map/jit(cholesky)/cholesky | solution.py:47
  525.9 9.8 %custom-call.34 = f32[1,128,128]{1,2,0:T(8,128)S(1)} custom-call(f32[1,128,128]{2,1,0:T(8,128)S(1)} %get-tuple-element.65), custom_call_target="InvertDiagBlocksLowerTriangular" | custom-call | tf_op jit(solution)/shard_map/jit(cholesky)/cholesky | solution.py:47
  536.5 11.9 %cholesky.253 = f32[128,128]{1,0:T(8,128)S(1)} custom-call(f32[128,128]{1,0:T(8,128)S(1)} %convolution_subtract_fusion.8), custom_call_target="Cholesky" | custom-call | tf_op jit(solution)/shard_map/jit(cholesky)/cholesky | solution.py:47
  554.9 11.3 %while.1 = (s32[]{:T(128)}, f32[512,512]{0,1:T(8,128)S(1)}, s32[4,2]{0,1:T(2,128)S(1)}, f32[4,128,128]{2,1,0:T(8,128)}, s32[]{:T(128)}) while((s32[]{:T(128)}, f32[512,512]{0,1:T(8,128)S(1)}, s32[4,2]{0,1:T(2,128)S(1)}, f32[4,128,128]{2,1,0:T(8,128)}, s32[]{:T(128)}) %tuple.42), condition=%wide.while_cond, body=%wide.while_body.sunk | while | flops 2 | bytes 393829 | solution.py:48
  566.3 40.2 %custom-call.35 = f32[4,128,128]{1,2,0:T(8,128)S(1)} custom-call(f32[4,128,128]{2,1,0:T(8,128)} %get-tuple-element.10), custom_call_target="InvertDiagBlocksLowerTriangular" | custom-call | tf_op jit(solution)/shard_map/triangular_solve | solution.py:48
  606.4 2.5 broadcast_multiply_fusion
  621.6 2.4 convolution_subtract_fusion.2
  625.0 3.0 fusion.14
  630.0 5.6 convolution_subtract_fusion.1
  636.3 3.6 convolution_subtract_fusion
  (156 shorter events, 81.3 us)
Async XLA Ops:
  7.2 88.2 %copy-start = (bf16[3,4,128,1024]{3,2,1,0:T(8,128)(2,1)S(1)}, bf16[3,4,128,1024]{3,2,1,0:T(8,128)(2,1)}, u32[]{:S(2)}) copy-start(bf16[3,4,128,1024]{3,2,1,0:T(8,128)(2,1)} %param.8) | copy-start | bytes 9437188
  7.2 63.3 %all-gather.3.cloned.1.call-start = ((), (), s32[]{:S(2)}) async-start(), calls=%async_computation.2 | async-start | bytes 5570560 | tf_op jit(solution)/shard_map/all_gather | solution.py:113
  124.9 2.0 copy-start.3
  129.7 21.3 %all-to-all-start = ((bf16[128,2,1024]{2,1,0:T(2,128)(2,1)}), bf16[128,2,1024]{2,1,0:T(2,128)(2,1)S(1)}, u32[]{:S(2)}, u32[]{:S(2)}) async-start(bf16[128,2,1024]{2,1,0:T(2,128)(2,1)} %reshape.290), calls=%async_computation | async-start | bytes 1048576 | tf_op jit(solution)/shard_map/all_to_all | solution.py:124
  151.0 68.9 %all-to-all-start.1 = ((bf16[128,128,64]{1,2,0:T(8,128)(2,1)}), bf16[128,128,64]{1,2,0:T(8,128)(2,1)S(1)}, u32[]{:S(2)}, u32[]{:S(2)}) async-start(bf16[128,128,64]{1,2,0:T(8,128)(2,1)} %bitcast.29), calls=%async_computation.1 | async-start | bytes 4194304 | tf_op jit(solution)/shard_map/all_to_all | solution.py:131
  155.7 310.9 %all-reduce.4.cloned.1.call-start = ((), (), s32[]{:S(2)}) async-start(), calls=%async_computation.4 | async-start | bytes 10485760 | tf_op jit(solution)/shard_map/psum | solution.py:65
  162.3 129.4 %copy-start.4 = (bf16[32,8192]{1,0:T(8,128)(2,1)}, bf16[32,8192]{1,0:T(8,128)(2,1)S(1)}, u32[]{:S(2)}) copy-start(bf16[32,8192]{1,0:T(8,128)(2,1)S(1)} %reshape.250) | copy-start | bytes 1572868
  162.3 34.0 %collective-permute-start = (bf16[32,8192]{1,0:T(8,128)(2,1)S(1)}, bf16[32,8192]{1,0:T(8,128)(2,1)S(1)}, u32[]{:S(2)}, u32[]{:S(2)}) collective-permute-start(bf16[32,8192]{1,0:T(8,128)(2,1)S(1)} %reshape.250), channel_id=1, source_target_pairs={{0,1},{1,2},{2,3},{3,4},{4,5},{5,6},{6,7},{7,8},{8,9},{9,10},{10,1... | collective-permute-start | bytes 1572872 | tf_op jit(solution)/shard_map/ppermute | solution.py:148
  164.0 32.3 %collective-permute-start.1 = (bf16[32,8192]{1,0:T(8,128)(2,1)S(1)}, bf16[32,8192]{1,0:T(8,128)(2,1)S(1)}, u32[]{:S(2)}, u32[]{:S(2)}) collective-permute-start(bf16[32,8192]{1,0:T(8,128)(2,1)S(1)} %reshape.250), channel_id=1, source_target_pairs={{0,15},{1,0},{2,1},{3,2},{4,3},{5,4},{6,5},{7,6},{8,7},{9,8},{10,9... | collective-permute-start | bytes 1572872 | tf_op jit(solution)/shard_map/ppermute | solution.py:153
  196.3 16.1 %collective-permute-start.2 = (bf16[32,8192]{1,0:T(8,128)(2,1)S(1)}, bf16[32,8192]{1,0:T(8,128)(2,1)}, u32[]{:S(2)}, u32[]{:S(2)}) collective-permute-start(bf16[32,8192]{1,0:T(8,128)(2,1)S(1)} %collective-permute-done), channel_id=1, source_target_pairs={{0,1},{1,2},{2,3},{3,4},{4,5},{5,6},{6,7},{7,8},{8,9},{9,10},{10,1... | collective-permute-start | bytes 1572872 | tf_op jit(solution)/shard_map/ppermute | solution.py:148
  196.3 16.1 %collective-permute-start.3 = (bf16[32,8192]{1,0:T(8,128)(2,1)S(1)}, bf16[32,8192]{1,0:T(8,128)(2,1)S(1)}, u32[]{:S(2)}, u32[]{:S(2)}) collective-permute-start(bf16[32,8192]{1,0:T(8,128)(2,1)S(1)} %collective-permute-done.1), channel_id=1, source_target_pairs={{0,15},{1,0},{2,1},{3,2},{4,3},{5,4},{6,5},{7,6},{8,7},{9,8},{10,9... | collective-permute-start | bytes 1572872 | tf_op jit(solution)/shard_map/ppermute | solution.py:153
  212.4 15.4 %collective-permute-start.4 = (bf16[32,8192]{1,0:T(8,128)(2,1)}, bf16[32,8192]{1,0:T(8,128)(2,1)}, u32[]{:S(2)}, u32[]{:S(2)}) collective-permute-start(bf16[32,8192]{1,0:T(8,128)(2,1)} %collective-permute-done.2), channel_id=1, source_target_pairs={{0,1},{1,2},{2,3},{3,4},{4,5},{5,6},{6,7},{7,8},{8,9},{9,10},{10,1... | collective-permute-start | bytes 1572872 | tf_op jit(solution)/shard_map/ppermute | solution.py:148
  212.4 15.6 %collective-permute-start.5 = (bf16[32,8192]{1,0:T(8,128)(2,1)S(1)}, bf16[32,8192]{1,0:T(8,128)(2,1)}, u32[]{:S(2)}, u32[]{:S(2)}) collective-permute-start(bf16[32,8192]{1,0:T(8,128)(2,1)S(1)} %collective-permute-done.3), channel_id=1, source_target_pairs={{0,15},{1,0},{2,1},{3,2},{4,3},{5,4},{6,5},{7,6},{8,7},{9,8},{10,9... | collective-permute-start | bytes 1572872 | tf_op jit(solution)/shard_map/ppermute | solution.py:153
  219.9 1.3 copy-start.5
  227.8 14.6 %collective-permute-start.6 = (bf16[32,8192]{1,0:T(8,128)(2,1)}, bf16[32,8192]{1,0:T(8,128)(2,1)S(1)}, u32[]{:S(2)}, u32[]{:S(2)}) collective-permute-start(bf16[32,8192]{1,0:T(8,128)(2,1)} %collective-permute-done.4), channel_id=1, source_target_pairs={{0,1},{1,2},{2,3},{3,4},{4,5},{5,6},{6,7},{7,8},{8,9},{9,10},{10,1... | collective-permute-start | bytes 1572872 | tf_op jit(solution)/shard_map/ppermute | solution.py:148
  228.0 14.4 %collective-permute-start.7 = (bf16[32,8192]{1,0:T(8,128)(2,1)}, bf16[32,8192]{1,0:T(8,128)(2,1)S(1)}, u32[]{:S(2)}, u32[]{:S(2)}) collective-permute-start(bf16[32,8192]{1,0:T(8,128)(2,1)} %collective-permute-done.5), channel_id=1, source_target_pairs={{0,15},{1,0},{2,1},{3,2},{4,3},{5,4},{6,5},{7,6},{8,7},{9,8},{10,9... | collective-permute-start | bytes 1572872 | tf_op jit(solution)/shard_map/ppermute | solution.py:153
  242.4 13.2 %collective-permute-start.8 = (bf16[32,8192]{1,0:T(8,128)(2,1)S(1)}, bf16[32,8192]{1,0:T(8,128)(2,1)S(1)}, u32[]{:S(2)}, u32[]{:S(2)}) collective-permute-start(bf16[32,8192]{1,0:T(8,128)(2,1)S(1)} %collective-permute-done.6), channel_id=1, source_target_pairs={{0,1},{1,2},{2,3},{3,4},{4,5},{5,6},{6,7},{7,8},{8,9},{9,10},{10,1... | collective-permute-start | bytes 1572872 | tf_op jit(solution)/shard_map/ppermute | solution.py:148
  242.4 13.2 %collective-permute-start.9 = (bf16[32,8192]{1,0:T(8,128)(2,1)S(1)}, bf16[32,8192]{1,0:T(8,128)(2,1)S(1)}, u32[]{:S(2)}, u32[]{:S(2)}) collective-permute-start(bf16[32,8192]{1,0:T(8,128)(2,1)S(1)} %collective-permute-done.7), channel_id=1, source_target_pairs={{0,15},{1,0},{2,1},{3,2},{4,3},{5,4},{6,5},{7,6},{8,7},{9,8},{10,9... | collective-permute-start | bytes 1572872 | tf_op jit(solution)/shard_map/ppermute | solution.py:153
  255.6 12.3 %collective-permute-start.10 = (bf16[32,8192]{1,0:T(8,128)(2,1)S(1)}, bf16[32,8192]{1,0:T(8,128)(2,1)S(1)}, u32[]{:S(2)}, u32[]{:S(2)}) collective-permute-start(bf16[32,8192]{1,0:T(8,128)(2,1)S(1)} %collective-permute-done.8), channel_id=1, source_target_pairs={{0,1},{1,2},{2,3},{3,4},{4,5},{5,6},{6,7},{7,8},{8,9},{9,10},{10,1... | collective-permute-start | bytes 1572872 | tf_op jit(solution)/shard_map/ppermute | solution.py:148
  255.6 12.3 %collective-permute-start.11 = (bf16[32,8192]{1,0:T(8,128)(2,1)S(1)}, bf16[32,8192]{1,0:T(8,128)(2,1)S(1)}, u32[]{:S(2)}, u32[]{:S(2)}) collective-permute-start(bf16[32,8192]{1,0:T(8,128)(2,1)S(1)} %collective-permute-done.9), channel_id=1, source_target_pairs={{0,15},{1,0},{2,1},{3,2},{4,3},{5,4},{6,5},{7,6},{8,7},{9,8},{10,9... | collective-permute-start | bytes 1572872 | tf_op jit(solution)/shard_map/ppermute | solution.py:153
  267.9 11.4 %collective-permute-start.12 = (bf16[32,8192]{1,0:T(8,128)(2,1)S(1)}, bf16[32,8192]{1,0:T(8,128)(2,1)S(1)}, u32[]{:S(2)}, u32[]{:S(2)}) collective-permute-start(bf16[32,8192]{1,0:T(8,128)(2,1)S(1)} %collective-permute-done.10), channel_id=1, source_target_pairs={{0,1},{1,2},{2,3},{3,4},{4,5},{5,6},{6,7},{7,8},{8,9},{9,10},{10,1... | collective-permute-start | bytes 1572872 | tf_op jit(solution)/shard_map/ppermute | solution.py:148
  267.9 12.2 %collective-permute-start.13 = (bf16[32,8192]{1,0:T(8,128)(2,1)S(1)}, bf16[32,8192]{1,0:T(8,128)(2,1)S(1)}, u32[]{:S(2)}, u32[]{:S(2)}) collective-permute-start(bf16[32,8192]{1,0:T(8,128)(2,1)S(1)} %collective-permute-done.11), channel_id=1, source_target_pairs={{0,15},{1,0},{2,1},{3,2},{4,3},{5,4},{6,5},{7,6},{8,7},{9,8},{10,9... | collective-permute-start | bytes 1572872 | tf_op jit(solution)/shard_map/ppermute | solution.py:153
  279.3 11.4 %collective-permute-start.14 = (bf16[32,8192]{1,0:T(8,128)(2,1)S(1)}, bf16[32,8192]{1,0:T(8,128)(2,1)S(1)}, u32[]{:S(2)}, u32[]{:S(2)}) collective-permute-start(bf16[32,8192]{1,0:T(8,128)(2,1)S(1)} %collective-permute-done.12), channel_id=1, source_target_pairs={{0,1},{1,2},{2,3},{3,4},{4,5},{5,6},{6,7},{7,8},{8,9},{9,10},{10,1... | collective-permute-start | bytes 1572872 | tf_op jit(solution)/shard_map/ppermute | solution.py:148
  297.6 1.0 copy-start.8
  307.6 322.4 %all-gather.5.cloned.1.call-start = ((), (), s32[]{:S(2)}) async-start(), calls=%async_computation.3 | async-start | bytes 8912896 | tf_op jit(solution)/shard_map/all_gather | solution.py:175
  466.6 1.8 copy-start.7
  566.3 48.2 %copy-start.6 = (f32[512,512]{0,1:T(8,128)}, f32[512,512]{0,1:T(8,128)S(1)}, u32[]{:S(2)}) copy-start(f32[512,512]{0,1:T(8,128)S(1)} %get-tuple-element.133) | copy-start | bytes 3145732
  630.0 6.4 copy-start.2
  636.3 3.6 copy-start.1
Sparse Core Ops, SparseCore 0:
  10.8 59.6 all-gather.2
  307.7 158.8 all-reduce.3
  468.7 69.3 all-gather.4
